TPU v7x, 32 devices: a whole 2x2x4 slice. The times are simulated.
32 devices in a mesh: band: 4 (over x, core), freq: 8 (over z, y).
Axes of the slice: x: 2, y: 2, z: 4, core: 2. Of those that a mesh axis runs over, the one named last changes fastest.
Arguments:
- samples: float32 [2048, 16384], P('band', 'freq'), may hold values from -6 to 6
- channel_delay: int32 [2048, 64], P('band'), may hold values from 0 to 4095
- merge_slope: int32 [7], replicated, may hold values from 16 to 1023
- tap_offset: int32 [32, 16], replicated, may hold values from -32 to 32, as said below
- tap_weight: float32 [32, 16], replicated, may hold values from -1.5 to 1.5
Outputs:
- best_power: float32 [512, 8192], P('band', 'freq')
Inputs may be any that keep to these rules, and one draw needn't show every extreme that they name: `tap_offset`: in every draw some template has a tap at offset -32 and some template has one at 32.
All inputs are finite; a program needn't handle non-finite values.
Results may differ from a plain program's by a relative error of at most 0.0003.
Values sent between devices are 32-bit elements; how exact they have to be, the bound alone decides.
A program may use at most 256 MiB of HBM per device.

v0:
```python
import functools
import math

import jax
import jax.numpy as jnp
import numpy as np
from jax import lax
from jax.experimental import pallas as pl
from jax.experimental.pallas import tpu as pltpu
from jax.sharding import PartitionSpec as P

REACH = 32
DELAY_BOUND = 4096
LANES = 128
GROUP = 8


two_pi = 2.0 * math.pi


def from_partner(value, axis, stride):
    return lax.ppermute(value, axis, [(i, i ^ 1 << stride) for i in range(lax.axis_size(axis))])


def extended(cells, sides, width):
    for axis, dim in sides:
        count = lax.axis_size(axis)
        ends = count - 1
        head = lax.slice_in_dim(cells, 0, width, axis=dim)
        tail = lax.slice_in_dim(cells, cells.shape[dim] - width, cells.shape[dim], axis=dim)
        cells = jnp.concatenate(
            [
                lax.ppermute(tail, axis, [(i, (i + 1) % count) for i in range(ends)]),
                cells,
                lax.ppermute(head, axis, [((i + 1) % count, i) for i in range(ends)]),
            ],
            axis=dim,
        )
    return cells


def turning(count, modulus):
    angle = (count % modulus).astype(jnp.float32) * (two_pi / modulus)
    return (jnp.cos(angle), jnp.sin(angle))


def rotate(real, imag, cosine, sine_part):
    return (real * cosine + imag * sine_part, imag * cosine - real * sine_part)


def merge_nodes(lower_half, upper_half, out_index, slopes, bins_index, modulus):
    shift = out_index[None, :] * slopes[:, None] // 16 % modulus
    cosine, sine_part = turning(shift[:, :, None] * bins_index[None, None, :], modulus)
    up_re, up_im = rotate(upper_half[0], upper_half[1], cosine, sine_part)
    return jnp.stack([lower_half[0] + up_re, lower_half[1] + up_im]) * (1.0 / math.sqrt(2.0))


def pick_entry(table, index):
    return jnp.sum(jnp.where(lax.iota(jnp.int32, table.shape[0]) == index, table, 0))


def shift_sum_kernel(delay_ref, series_ref, out_ref, rows_ref, window_ref):
    step = pl.program_id(0)
    parts, _, part_len = series_ref.shape
    outer = part_len // LANES
    count = parts * outer
    turns = DELAY_BOUND // LANES
    for part in range(parts):
        for block in range(outer):
            rows_ref[pl.ds((part * outer + block) * GROUP, GROUP), :] = series_ref[
                part, :, block * LANES : (block + 1) * LANES
            ]

    for chan in range(GROUP):
        grid = rows_ref[pl.ds(chan, count, stride=GROUP), :].T
        for turn in range(turns + 1):
            shift = (turns - turn) % count
            window_ref[chan, turn * LANES : (turn + 1) * LANES, :] = (
                pltpu.roll(grid, shift, 1) if shift else grid
            )

    @pl.when(step == 0)
    def _():
        out_ref[...] = jnp.zeros_like(out_ref)

    def one_delay(delay_no, carry):
        total = out_ref[delay_no]
        for chan in range(GROUP):
            start = DELAY_BOUND - delay_ref[step * GROUP + chan, delay_no]
            total = total + window_ref[chan, pl.ds(start, LANES), :]
        out_ref[delay_no] = total
        return carry

    lax.fori_loop(0, out_ref.shape[0], one_delay, 0)


def shift_sum(delays, series):
    parts, chan_count, part_len = series.shape
    delay_count = delays.shape[1]
    count = parts * part_len // LANES
    return pl.pallas_call(
        shift_sum_kernel,
        out_shape=jax.ShapeDtypeStruct((delay_count, LANES, count), jnp.float32),
        grid_spec=pltpu.PrefetchScalarGridSpec(
            num_scalar_prefetch=1,
            grid=(chan_count // GROUP,),
            in_specs=[pl.BlockSpec((parts, GROUP, part_len), lambda i, _: (0, i, 0))],
            out_specs=pl.BlockSpec((delay_count, LANES, count), lambda i, _: (0, 0, 0)),
            scratch_shapes=[
                pltpu.VMEM((count * GROUP, LANES), jnp.float32),
                pltpu.VMEM((GROUP, DELAY_BOUND + LANES, count), jnp.float32),
            ],
        ),
        compiler_params=pltpu.CompilerParams(vmem_limit_bytes=48 << 20),
        name="shift_sum",
    )(delays, series)


def dft_kernel(first_ref, twist_cos_ref, twist_sin_ref, second_ref, parts_ref, out_ref):
    grid = parts_ref[0, 0]
    for part in range(1, parts_ref.shape[0]):
        grid = grid + parts_ref[part, 0]
    count = grid.shape[1]
    top = lax.Precision.HIGHEST
    part_out = jnp.dot(grid, first_ref[...], precision=top, preferred_element_type=jnp.float32)
    real, imag = rotate(
        part_out[:, :count], part_out[:, count:], twist_cos_ref[...], twist_sin_ref[...]
    )
    both = jnp.concatenate([real, imag], axis=0)
    spectrum = jnp.dot(second_ref[...], both, precision=top, preferred_element_type=jnp.float32)
    slabs, _, _, rows, _ = out_ref.shape
    half = slabs * rows
    for slab in range(slabs):
        out_ref[slab, 0, 0] = spectrum[slab * rows : (slab + 1) * rows]
        out_ref[slab, 1, 0] = spectrum[half + slab * rows : half + (slab + 1) * rows]


def dft(parts, slabs, scale):
    part_count, row_count, inner, outer = parts.shape
    length = inner * outer
    kept = inner // 2
    rows = kept // slabs
    index = np.arange(outer)
    angle = (index[:, None] * index[None, :] % outer) * (two_pi / outer)
    first = np.concatenate([np.cos(angle), -np.sin(angle)], axis=1)
    angle = (np.arange(inner)[:, None] * index[None, :]) * (two_pi / length)
    twist_cos, twist_sin = np.cos(angle), np.sin(angle)
    angle = (np.arange(kept)[:, None] * np.arange(inner)[None, :] % inner) * (two_pi / inner)
    cosine, sine_part = np.cos(angle) * scale, np.sin(angle) * scale
    second = np.block([[cosine, sine_part], [-sine_part, cosine]])
    tables = [jnp.asarray(t, jnp.float32) for t in (first, twist_cos, twist_sin, second)]
    whole = [pl.BlockSpec(t.shape, lambda i: (0, 0)) for t in tables]
    return pl.pallas_call(
        dft_kernel,
        out_shape=jax.ShapeDtypeStruct((slabs, 2, row_count, rows, outer), jnp.float32),
        grid=(row_count,),
        in_specs=whole
        + [pl.BlockSpec((part_count, 1, inner, outer), lambda i: (0, i, 0, 0))],
        out_specs=pl.BlockSpec((slabs, 2, 1, rows, outer), lambda i: (0, 0, i, 0, 0)),
        name="dft",
    )(*tables, parts)


def split_halves(value):
    coarse = value.astype(jnp.bfloat16)
    fine = (value - coarse.astype(jnp.float32)).astype(jnp.bfloat16)
    return coarse, fine


def template_kernel(profile_ref, left_ref, right_ref, out_ref, bank_ref):
    template_count, width = profile_ref.shape

    @pl.when(pl.program_id(0) == 0)
    def _():
        def one_template(template_no, carry):
            row = jnp.broadcast_to(profile_ref[pl.ds(template_no, 1), :], (LANES, width))
            coarse, fine = split_halves(pltpu.roll(row, 0, 1, stride=1, stride_axis=0))
            where = pl.ds(pl.multiple_of(template_no * LANES, LANES), LANES)
            bank_ref[where, :] = jnp.concatenate([coarse, coarse, fine], axis=1)
            return carry

        lax.fori_loop(0, template_count, one_template, 0)

    coarse, fine = split_halves(jnp.concatenate([left_ref[...], right_ref[...]], axis=1))
    cells = jnp.concatenate([coarse, fine, coarse], axis=1)
    rows = out_ref.shape[0]
    best = jnp.zeros_like(out_ref)
    for pair in range(template_count // 2):
        corr = lax.dot_general(
            cells,
            bank_ref[pair * 2 * LANES : (pair + 1) * 2 * LANES, :],
            (((1,), (1,)), ((), ())),
            preferred_element_type=jnp.float32,
        )
        power = corr[:rows] * corr[:rows] + corr[rows:] * corr[rows:]
        best = jnp.maximum(best, jnp.maximum(power[:, :LANES], power[:, LANES:]))
    out_ref[...] = best


def template_search(profile, cells, bins_dev):
    rows = cells.shape[0] // 2
    template_count, width = profile.shape
    return pl.pallas_call(
        template_kernel,
        out_shape=jax.ShapeDtypeStruct((rows, bins_dev), jnp.float32),
        grid=(bins_dev // LANES,),
        in_specs=[
            pl.BlockSpec((template_count, width), lambda i: (0, 0)),
            pl.BlockSpec((2 * rows, LANES), lambda i: (0, i)),
            pl.BlockSpec((2 * rows, LANES), lambda i: (0, i + 1)),
        ],
        out_specs=pl.BlockSpec((rows, LANES), lambda i: (0, i)),
        scratch_shapes=[pltpu.VMEM((template_count * LANES, 3 * width), jnp.bfloat16)],
        compiler_params=pltpu.CompilerParams(vmem_limit_bytes=48 << 20),
        name="template_search",
    )(profile, cells, cells)


def per_device(samples, channel_delay, merge_slope, tap_offset, tap_weight):
    freq_count = lax.axis_size("freq")
    band_count = lax.axis_size("band")
    band_pos = lax.axis_index("band")
    freq_pos = lax.axis_index("freq")
    chan_dev, samp_dev = samples.shape
    length = samp_dev * freq_count
    bins_dev = length // 2 // freq_count
    delays_sub = channel_delay.shape[1]
    block_rows = 2 * delays_sub
    per_sub = chan_dev // 2
    chan_own = chan_dev // freq_count
    share = per_sub // chan_own
    bins_index = freq_pos * bins_dev + lax.iota(jnp.int32, bins_dev)

    series = lax.all_to_all(
        samples.reshape(freq_count, chan_own, samp_dev), "freq", split_axis=0, concat_axis=0, tiled=True
    )
    own_delay = lax.dynamic_slice_in_dim(channel_delay, freq_pos * chan_own, chan_own, axis=0)
    partial = shift_sum(own_delay, series)
    inner, outer = partial.shape[1:]
    groups = [list(range(g * share, (g + 1) * share)) for g in range(freq_count // share)]
    parts = lax.all_to_all(
        partial.reshape(share, delays_sub // share, inner, outer),
        "freq", split_axis=0, concat_axis=0, axis_index_groups=groups, tiled=True,
    )
    slabs = dft(parts, freq_count, 1.0 / math.sqrt(length * per_sub))
    slabs = lax.all_to_all(slabs, "freq", split_axis=0, concat_axis=0, tiled=True)
    subband_sums = (
        slabs.reshape(2, share, 2, delays_sub // share, bins_dev)
        .transpose(2, 0, 1, 3, 4)
        .reshape(2, 2, delays_sub, bins_dev)
    )
    lower_half = jnp.concatenate([subband_sums[:, 0:1], subband_sums[:, 0:1]], axis=2)
    upper_half = jnp.concatenate([subband_sums[:, 1:2], subband_sums[:, 1:2]], axis=2)
    first_slope = pick_entry(merge_slope, 2 * band_pos).reshape(1)
    level_zero = merge_nodes(
        lower_half, upper_half, lax.iota(jnp.int32, block_rows), first_slope, bins_index, length
    )
    section_count = band_count.bit_length() - 1
    current = level_zero
    for section_no in range(1, section_count + 1):
        group_size = 1 << section_no
        half_size = group_size >> 1
        position = band_pos % group_size
        partner = from_partner(current, "band", section_no - 1)
        upper_side = position >= half_size
        lower_half = jnp.where(upper_side, partner, current)
        upper_half = jnp.where(upper_side, current, partner)
        node_no = band_pos // group_size
        section_slope = pick_entry(
            merge_slope, node_no * (2 * group_size) + group_size - 1
        ).reshape(1)
        out_index = position * block_rows + lax.iota(jnp.int32, block_rows)
        current = merge_nodes(lower_half, upper_half, out_index, section_slope, bins_index, length)
    spectra = current[:, 0]
    bordered = extended(spectra, (("freq", 2),), REACH)
    width = 2 * LANES
    span = lax.iota(jnp.int32, width)
    matches = tap_offset[:, :, None] + REACH == span[None, None, :]
    profile = jnp.sum(jnp.where(matches, tap_weight[:, :, None], 0.0), axis=1)
    cells = jnp.pad(bordered, ((0, 0), (0, 0), (0, LANES - 2 * REACH)))
    return template_search(profile, cells.reshape(2 * block_rows, bins_dev + LANES), bins_dev)


def solution(mesh):
    placed = (P("band", "freq"), P("band", None), P(), P(), P())
    return jax.shard_map(
        per_device, mesh=mesh, in_specs=placed, out_specs=P("band", "freq"), check_vma=False
    )
```

profile of v0, /device:TPU:0, one launch (start us, length us, event | category | flops | bytes accessed | tf_op | source)
XLA Modules:
  0.0 326.0 jit_solution(6692760061963836809)
XLA Ops:
  0.0 7.4 %all-to-all-start = ((f32[8,64,2048]{2,1,0:T(8,128)}), f32[8,64,2048]{2,1,0:T(8,128)}, u32[]{:S(2)}, u32[]{:S(2)}) async-start(f32[8,64,2048]{2,1,0:T(8,128)} %bitcast.14), calls=%async_computation | async-start | bytes 8388608 | tf_op jit(solution)/shard_map/all_to_all | solution.py:234
  7.6 93.1 %all-to-all-done.series_ref = f32[8,64,2048]{2,1,0:T(8,128)} async-done(((f32[8,64,2048]{2,1,0:T(8,128)}), f32[8,64,2048]{2,1,0:T(8,128)}, u32[]{:S(2)}, u32[]{:S(2)}) %all-to-all-start) | async-done | bytes 4194336 | tf_op jit(solution)/shard_map/all_to_all | solution.py:234
  100.7 63.4 %shift_sum.1 = f32[64,128,128]{2,1,0:T(8,128)S(1)} custom-call(s32[64,64]{1,0:T(8,128)S(1)} %copy.18.delay_ref, f32[8,64,2048]{2,1,0:T(8,128)} %all-to-all-done.series_ref), custom_call_target="tpu_custom_call" | custom-call | tf_op jit(solution)/shard_map/shift_sum/pallas_call | solution.py:101
  164.2 50.4 %all_to_all.15.parts_ref = f32[4,16,128,128]{3,2,1,0:T(8,128)} all-to-all(f32[4,16,128,128]{3,2,1,0:T(8,128)S(1)} %bitcast.11), channel_id=1, replica_groups={{0,1,2,3},{4,5,6,7},{8,9,10,11},{12,13,14,15},{16,17,18,19},{20,21,22,2..., dimensions={0} | all-to-all | bytes 8388608 | tf_op jit(solution)/shard_map/all_to_all | solution.py:241
  214.6 14.8 %dft.1 = f32[8,2,16,8,128]{4,3,2,1,0:T(8,128)} custom-call(f32[128,256]{1,0:T(8,128)} %constant.151.clone.first_ref, f32[128,128]{1,0:T(8,128)} %constant.152.clone.twist_cos_ref, f32[128,128]{1,0:T(8,128)} %constant.153.clone.twist_sin_ref, f32[128,256]{1,0:T(8,128)} %constant.154.clone.second_ref, f32[4,16,128,128]{3,2,1,0:T(8,128)} %all_to_all.15.parts_ref), custom_call_target="tpu_custom_call" | custom-call | tf_op jit(solution)/shard_map/dft/pallas_call | solution.py:153
  229.4 3.7 %all-to-all-start.2 = ((f32[8,2,16,8,128]{4,3,2,1,0:T(8,128)}), f32[8,2,16,8,128]{4,3,2,1,0:T(8,128)S(1)}, u32[]{:S(2)}, u32[]{:S(2)}) async-start(f32[8,2,16,8,128]{4,3,2,1,0:T(8,128)} %dft.1), calls=%async_computation.2 | async-start | bytes 2097152 | tf_op jit(solution)/shard_map/all_to_all | solution.py:246
  233.1 0.7 fusion.23
  233.9 0.6 and_select_fusion.4
  234.5 24.2 %all-to-all-done.2 = f32[8,2,16,8,128]{4,3,2,1,0:T(8,128)S(1)} async-done(((f32[8,2,16,8,128]{4,3,2,1,0:T(8,128)}), f32[8,2,16,8,128]{4,3,2,1,0:T(8,128)S(1)}, u32[]{:S(2)}, u32[]{:S(2)}) %all-to-all-start.2) | async-done | bytes 1048608 | tf_op jit(solution)/shard_map/all_to_all | solution.py:246
  259.0 2.8 fusion.11
  262.1 0.7 and_select_fusion.2
  262.8 1.9 collective-permute-done
  264.9 2.6 slice_add_fusion.3
  267.7 1.6 collective-permute-start.1
  269.4 0.7 and_select_fusion
  270.1 22.8 %collective-permute-done.1 = f32[2,1,128,1024]{3,2,1,0:T(8,128)S(1)} collective-permute-done((f32[2,1,128,1024]{3,2,1,0:T(8,128)S(1)}, f32[2,1,128,1024]{3,2,1,0:T(8,128)S(1)}, u32[]{:S(2)}, u32[]{:S(2)}) %collective-permute-start.1) | collective-permute-done | bytes 1048608 | tf_op jit(solution)/shard_map/ppermute | solution.py:22
  293.2 2.6 fusion.13
  296.0 3.2 collective-permute-start.2
  299.2 1.3 collective-permute-start.3
  300.5 0.3 select_reduce_fusion.profile_ref
  300.7 0.9 collective-permute-done.2
  301.7 4.4 %collective-permute-done.3 = f32[2,128,32]{2,1,0:T(8,128)S(1)} collective-permute-done((f32[2,128,32]{2,1,0:T(8,128)S(1)}, f32[2,128,32]{2,1,0:T(8,128)S(1)}, u32[]{:S(2)}, u32[]{:S(2)}) %collective-permute-start.3) | collective-permute-done | bytes 32800 | tf_op jit(solution)/shard_map/ppermute | solution.py:35
  306.0 0.8 concatenate.30
  306.9 19.1 %template_search.1 = f32[128,1024]{1,0:T(8,128)} custom-call(f32[32,256]{1,0:T(8,128)S(1)} %select_reduce_fusion.profile_ref, f32[256,1152]{1,0:T(8,128)S(1)} %bitcast.12, f32[256,1152]{1,0:T(8,128)S(1)} %bitcast.13), custom_call_target="tpu_custom_call" | custom-call | tf_op jit(solution)/shard_map/template_search/pallas_call | solution.py:203
  (25 shorter events, 1.8 us)
Async XLA Ops:
  0.0 7.4 %copy-start = (s32[512,64]{0,1:T(8,128)S(1)}, s32[512,64]{0,1:T(8,128)}, u32[]{:S(2)}) copy-start(s32[512,64]{0,1:T(8,128)} %param.10) | copy-start | bytes 393220
  0.0 100.7 %all-to-all-start = ((f32[8,64,2048]{2,1,0:T(8,128)}), f32[8,64,2048]{2,1,0:T(8,128)}, u32[]{:S(2)}, u32[]{:S(2)}) async-start(f32[8,64,2048]{2,1,0:T(8,128)} %bitcast.14), calls=%async_computation | async-start | bytes 8388608 | tf_op jit(solution)/shard_map/all_to_all | solution.py:234
  214.6 18.5 %copy-start.3 = (s32[7]{0:T(128)S(1)}, s32[7]{0:T(128)}, u32[]{:S(2)}) copy-start(s32[7]{0:T(128)} %param.11) | copy-start | bytes 88
  229.4 29.3 %all-to-all-start.2 = ((f32[8,2,16,8,128]{4,3,2,1,0:T(8,128)}), f32[8,2,16,8,128]{4,3,2,1,0:T(8,128)S(1)}, u32[]{:S(2)}, u32[]{:S(2)}) async-start(f32[8,2,16,8,128]{4,3,2,1,0:T(8,128)} %dft.1), calls=%async_computation.2 | async-start | bytes 2097152 | tf_op jit(solution)/shard_map/all_to_all | solution.py:246
  262.0 2.7 collective-permute-start
  262.8 6.5 %copy-start.2 = (s32[32,16]{0,1:T(8,128)S(1)}, s32[32,16]{0,1:T(8,128)}, u32[]{:S(2)}) copy-start(s32[32,16]{0,1:T(8,128)} %param.12) | copy-start | bytes 6148
  262.8 6.6 %copy-start.1 = (f32[32,16]{0,1:T(8,128)S(1)}, f32[32,16]{0,1:T(8,128)}, u32[]{:S(2)}) copy-start(f32[32,16]{0,1:T(8,128)} %param.13) | copy-start | bytes 6148
  267.7 25.3 %collective-permute-start.1 = (f32[2,1,128,1024]{3,2,1,0:T(8,128)S(1)}, f32[2,1,128,1024]{3,2,1,0:T(8,128)S(1)}, u32[]{:S(2)}, u32[]{:S(2)}) collective-permute-start(f32[2,1,128,1024]{3,2,1,0:T(8,128)S(1)} %maximum_multiply_fusion.1), channel_id=1, source_target_pairs={{0,16},{8,24},{16,0},{24,8},{1,17},{9,25},{17,1},{25,9},{2,18},{10... | collective-permute-start | bytes 3145736 | tf_op jit(solution)/shard_map/ppermute | solution.py:22
  296.0 5.7 %collective-permute-start.2 = (f32[2,128,32]{2,1,0:T(8,128)S(1)}, f32[2,128,32]{2,1,0:T(8,128)S(1)}, u32[]{:S(2)}, u32[]{:S(2)}) collective-permute-start(f32[2,128,32]{2,1,0:T(8,128)S(1)} %get-tuple-element.19), channel_id=1, source_target_pairs={{0,1},{1,2},{2,3},{3,4},{4,5},{5,6},{6,7},{8,9},{9,10},{10,11},{11... | collective-permute-start | bytes 98312 | tf_op jit(solution)/shard_map/ppermute | solution.py:33
  299.2 6.9 %collective-permute-start.3 = (f32[2,128,32]{2,1,0:T(8,128)S(1)}, f32[2,128,32]{2,1,0:T(8,128)S(1)}, u32[]{:S(2)}, u32[]{:S(2)}) collective-permute-start(f32[2,128,32]{2,1,0:T(8,128)S(1)} %get-tuple-element.18), channel_id=1, source_target_pairs={{1,0},{2,1},{3,2},{4,3},{5,4},{6,5},{7,6},{9,8},{10,9},{11,10},{12... | collective-permute-start | bytes 98312 | tf_op jit(solution)/shard_map/ppermute | solution.py:35
where the time goes:
time: 327 us; the launch traced here: 326 us
  waiting for transfers between devices  147 us (45%)
  Pallas kernels  97.4 us (30%)
  blocking collectives  50.4 us (15%)
  starting transfers between devices  17.3 us (5%)
  other arithmetic  11.8 us (4%)
    all_to_all x1, waiting for transfers between devices, per_device(): lax.all_to_all(samples.reshape(freq_count, chan_own, samp_dev), 'freq', s...  93.1 us
    pallas_call x1, Pallas kernels, shift_sum(): pl.pallas_call(shift_sum_kernel, out_shape=jax.ShapeDtypeStruct((delay_co...  63.4 us
    all_to_all x1, blocking collectives, per_device(): lax.all_to_all(partial.reshape(share, delays_sub // share, inner, outer),...  50.4 us
    ppermute x2, waiting for transfers between devices, from_partner(): lax.ppermute(value, axis, [(i, i ^ 1 << stride) for i in range(lax.axis_s...  24.7 us
    all_to_all x1, waiting for transfers between devices, per_device(): lax.all_to_all(slabs, 'freq', split_axis=0, concat_axis=0, tiled=True)  24.2 us
    pallas_call x1, Pallas kernels, template_search(): pl.pallas_call(template_kernel, out_shape=jax.ShapeDtypeStruct((rows, bin...  19.1 us
    pallas_call x1, Pallas kernels, dft(): pl.pallas_call(dft_kernel, out_shape=jax.ShapeDtypeStruct((slabs, 2, row_...  14.8 us
    all_to_all x1, starting transfers between devices, per_device(): lax.all_to_all(samples.reshape(freq_count, chan_own, samp_dev), 'freq', s...  7.44 us
  transfers between devices with their start and end apart: 6, of which 6 were waited for; matrix products, arithmetic and copies ran while one was open for 1% of the time, Pallas kernels for 0%

commit v1 on v0

--- a/solution.py
+++ b/solution.py
@@ -59,7 +59,9 @@
     return jnp.sum(jnp.where(lax.iota(jnp.int32, table.shape[0]) == index, table, 0))
 
 
-def shift_sum_kernel(delay_ref, series_ref, out_ref, rows_ref, window_ref):
+def shift_sum_kernel(has_base, delay_ref, series_ref, *refs):
+    base_ref = refs[0] if has_base else None
+    out_ref, rows_ref, window_ref = refs[has_base:]
     step = pl.program_id(0)
     parts, _, part_len = series_ref.shape
     outer = part_len // LANES
@@ -81,7 +83,7 @@
 
     @pl.when(step == 0)
     def _():
-        out_ref[...] = jnp.zeros_like(out_ref)
+        out_ref[...] = base_ref[...] if has_base else jnp.zeros_like(out_ref)
 
     def one_delay(delay_no, carry):
         total = out_ref[delay_no]
@@ -94,40 +96,85 @@
     lax.fori_loop(0, out_ref.shape[0], one_delay, 0)
 
 
-def shift_sum(delays, series):
+def shift_sum(delays, series, base):
     parts, chan_count, part_len = series.shape
     delay_count = delays.shape[1]
     count = parts * part_len // LANES
+    has_base = base is not None
+    block = pl.BlockSpec((delay_count, LANES, count), lambda i, _: (0, 0, 0))
     return pl.pallas_call(
-        shift_sum_kernel,
+        functools.partial(shift_sum_kernel, int(has_base)),
         out_shape=jax.ShapeDtypeStruct((delay_count, LANES, count), jnp.float32),
         grid_spec=pltpu.PrefetchScalarGridSpec(
             num_scalar_prefetch=1,
             grid=(chan_count // GROUP,),
-            in_specs=[pl.BlockSpec((parts, GROUP, part_len), lambda i, _: (0, i, 0))],
-            out_specs=pl.BlockSpec((delay_count, LANES, count), lambda i, _: (0, 0, 0)),
+            in_specs=[pl.BlockSpec((parts, GROUP, part_len), lambda i, _: (0, i, 0))]
+            + [block] * has_base,
+            out_specs=block,
             scratch_shapes=[
                 pltpu.VMEM((count * GROUP, LANES), jnp.float32),
                 pltpu.VMEM((GROUP, DELAY_BOUND + LANES, count), jnp.float32),
             ],
         ),
+        input_output_aliases={2: 0} if has_base else {},
+        cost_estimate=pl.CostEstimate(
+            flops=1000 * chan_count * parts * part_len * delay_count // 8,
+            bytes_accessed=4 * (series.size + delay_count * LANES * count),
+            transcendentals=0,
+        ),
         compiler_params=pltpu.CompilerParams(vmem_limit_bytes=48 << 20),
         name="shift_sum",
-    )(delays, series)
-
-
-def dft_kernel(first_ref, twist_cos_ref, twist_sin_ref, second_ref, parts_ref, out_ref):
-    grid = parts_ref[0, 0]
-    for part in range(1, parts_ref.shape[0]):
-        grid = grid + parts_ref[part, 0]
-    count = grid.shape[1]
-    top = lax.Precision.HIGHEST
-    part_out = jnp.dot(grid, first_ref[...], precision=top, preferred_element_type=jnp.float32)
+    )(delays, series, *([base] if has_base else []))
+
+
+def chunk_sizes(group_count):
+    if group_count < 8:
+        return [1] * group_count if group_count <= 4 else [group_count - 3, 1, 1, 1]
+    last = group_count // 8
+    return [group_count - 5 * last, 2 * last, 2 * last, last]
+
+
+def reduce_halving(value, pos, bits):
+    left = sorted(bits, reverse=True)
+    for bit in bits:
+        dim = left.index(bit)
+        mine = pos >> bit & 1
+        kept = lax.dynamic_index_in_dim(value, mine, dim, keepdims=False)
+        sent = lax.dynamic_index_in_dim(value, 1 - mine, dim, keepdims=False)
+        value = kept + from_partner(sent, "freq", bit)
+        left.remove(bit)
+    return value
+
+
+def split_halves(value):
+    coarse = value.astype(jnp.bfloat16)
+    fine = (value - coarse.astype(jnp.float32)).astype(jnp.bfloat16)
+    return coarse, fine
+
+
+def table_halves(table, dim):
+    coarse = table.astype(jnp.bfloat16)
+    fine = (table - coarse.astype(np.float64)).astype(jnp.bfloat16)
+    return jnp.asarray(np.concatenate([coarse, coarse, fine], axis=dim))
+
+
+def dft_kernel(first_ref, twist_cos_ref, twist_sin_ref, second_ref, series_ref, out_ref):
+    count = series_ref.shape[2]
+    coarse, fine = split_halves(series_ref[0])
+    part_out = jnp.dot(
+        jnp.concatenate([coarse, fine, coarse], axis=1),
+        first_ref[...],
+        preferred_element_type=jnp.float32,
+    )
     real, imag = rotate(
         part_out[:, :count], part_out[:, count:], twist_cos_ref[...], twist_sin_ref[...]
     )
-    both = jnp.concatenate([real, imag], axis=0)
-    spectrum = jnp.dot(second_ref[...], both, precision=top, preferred_element_type=jnp.float32)
+    coarse, fine = split_halves(jnp.concatenate([real, imag], axis=0))
+    spectrum = jnp.dot(
+        second_ref[...],
+        jnp.concatenate([coarse, fine, coarse], axis=0),
+        preferred_element_type=jnp.float32,
+    )
     slabs, _, _, rows, _ = out_ref.shape
     half = slabs * rows
     for slab in range(slabs):
@@ -135,8 +182,8 @@
         out_ref[slab, 1, 0] = spectrum[half + slab * rows : half + (slab + 1) * rows]
 
 
-def dft(parts, slabs, scale):
-    part_count, row_count, inner, outer = parts.shape
+def dft(series, slabs, scale):
+    row_count, inner, outer = series.shape
     length = inner * outer
     kept = inner // 2
     rows = kept // slabs
@@ -148,23 +195,18 @@
     angle = (np.arange(kept)[:, None] * np.arange(inner)[None, :] % inner) * (two_pi / inner)
     cosine, sine_part = np.cos(angle) * scale, np.sin(angle) * scale
     second = np.block([[cosine, sine_part], [-sine_part, cosine]])
-    tables = [jnp.asarray(t, jnp.float32) for t in (first, twist_cos, twist_sin, second)]
+    first, second = table_halves(first, 0), table_halves(second, 1)
+    tables = [first, jnp.asarray(twist_cos, jnp.float32), jnp.asarray(twist_sin, jnp.float32), second]
     whole = [pl.BlockSpec(t.shape, lambda i: (0, 0)) for t in tables]
     return pl.pallas_call(
         dft_kernel,
         out_shape=jax.ShapeDtypeStruct((slabs, 2, row_count, rows, outer), jnp.float32),
         grid=(row_count,),
         in_specs=whole
-        + [pl.BlockSpec((part_count, 1, inner, outer), lambda i: (0, i, 0, 0))],
+        + [pl.BlockSpec((1, inner, outer), lambda i: (i, 0, 0))],
         out_specs=pl.BlockSpec((slabs, 2, 1, rows, outer), lambda i: (0, 0, i, 0, 0)),
         name="dft",
-    )(*tables, parts)
-
-
-def split_halves(value):
-    coarse = value.astype(jnp.bfloat16)
-    fine = (value - coarse.astype(jnp.float32)).astype(jnp.bfloat16)
-    return coarse, fine
+    )(*tables, series)
 
 
 def template_kernel(profile_ref, left_ref, right_ref, out_ref, bank_ref):
@@ -231,22 +273,36 @@
     share = per_sub // chan_own
     bins_index = freq_pos * bins_dev + lax.iota(jnp.int32, bins_dev)
 
-    series = lax.all_to_all(
-        samples.reshape(freq_count, chan_own, samp_dev), "freq", split_axis=0, concat_axis=0, tiled=True
-    )
     own_delay = lax.dynamic_slice_in_dim(channel_delay, freq_pos * chan_own, chan_own, axis=0)
-    partial = shift_sum(own_delay, series)
+    by_owner = samples.reshape(freq_count, chan_own, samp_dev)
+    start, waiting, previous, partial = 0, None, None, None
+    for groups in chunk_sizes(chan_own // GROUP):
+        end = start + groups * GROUP
+        chunk = by_owner[:, start:end]
+        if previous is not None:
+            chunk, previous = lax.optimization_barrier((chunk, previous))
+        series = lax.all_to_all(chunk, "freq", split_axis=0, concat_axis=0, tiled=True)
+        if waiting is not None:
+            previous = partial = shift_sum(*waiting, partial)
+        waiting = own_delay[start:end], series
+        start = end
+    partial = shift_sum(*waiting, partial)
+
     inner, outer = partial.shape[1:]
-    groups = [list(range(g * share, (g + 1) * share)) for g in range(freq_count // share)]
-    parts = lax.all_to_all(
-        partial.reshape(share, delays_sub // share, inner, outer),
-        "freq", split_axis=0, concat_axis=0, axis_index_groups=groups, tiled=True,
-    )
-    slabs = dft(parts, freq_count, 1.0 / math.sqrt(length * per_sub))
+    bits = list(range(share.bit_length() - 1))
+    rows = delays_sub // (2 * share)
+    streams = partial.reshape([2] + [2] * len(bits) + [rows, inner, outer])
+    owned = jnp.concatenate(
+        [
+            reduce_halving(streams[0], freq_pos, bits),
+            reduce_halving(streams[1], freq_pos, bits[::-1]),
+        ]
+    )
+    slabs = dft(owned, freq_count, 1.0 / math.sqrt(length * per_sub))
     slabs = lax.all_to_all(slabs, "freq", split_axis=0, concat_axis=0, tiled=True)
     subband_sums = (
-        slabs.reshape(2, share, 2, delays_sub // share, bins_dev)
-        .transpose(2, 0, 1, 3, 4)
+        slabs.reshape(2, share, 2, 2, rows, bins_dev)
+        .transpose(2, 0, 3, 1, 4, 5)
         .reshape(2, 2, delays_sub, bins_dev)
     )
     lower_half = jnp.concatenate([subband_sums[:, 0:1], subband_sums[:, 0:1]], axis=2)

time: 327 us -> 301 us (0.920)
  blocking collectives: 50.4 us -> 0 us
  waiting for transfers between devices: 147 us -> 120 us
  local copies, waits for them, and re-layouts: 1.62 us -> 27.6 us
  starting transfers between devices: 17.3 us -> 37.9 us
  other arithmetic: 11.8 us -> 15.7 us
    all_to_all x1 -> x4, waiting for transfers between devices: 93.1 us -> 36.7 us  [per_device(): lax.all_to_all(chunk, 'freq', split_axis=0, concat_axis=0, tiled=True)]
    all_to_all x1 -> x0, blocking collectives: 50.4 us -> none  [per_device(): lax.all_to_all(partial.reshape(share, delays_sub // share, inner, outer),...]
    ppermute x2 -> x6, waiting for transfers between devices: 24.7 us -> 55.8 us  [from_partner(): lax.ppermute(value, axis, [(i, i ^ 1 << stride) for i in range(lax.axis_s...]
    unnamed x10 -> x31, local copies, waits for them, and re-layouts: 0.17 us -> 16.7 us
    all_to_all x1 -> x4, starting transfers between devices: 7.44 us -> 20.6 us  [per_device(): lax.all_to_all(chunk, 'freq', split_axis=0, concat_axis=0, tiled=True)]
    slice x0 -> x7, local copies, waits for them, and re-layouts: none -> 8.28 us  [the longest x3 7.76 us: per_device(): chunk = by_owner[:, start:end]]
    ppermute x2 -> x6, starting transfers between devices: 1.69 us -> 8.27 us  [from_partner(): lax.ppermute(value, axis, [(i, i ^ 1 << stride) for i in range(lax.axis_s...]
    pallas_call x1 -> x4, Pallas kernels: 63.4 us -> 66.2 us  [shift_sum(): pl.pallas_call(functools.partial(shift_sum_kernel, int(has_base)), out_sh...]
  transfers between devices with their start and end apart: 6 -> 13, of which waited for: 6 -> 10; matrix products, arithmetic and copies ran while one was open for 1% -> 4% of each run, Pallas kernels for 0% -> 19%
where the time goes in v1:
time: 301 us; the launch traced here: 299 us
  waiting for transfers between devices  120 us (40%)
  Pallas kernels  97.5 us (32%)
  starting transfers between devices  37.9 us (13%)
  local copies, waits for them, and re-layouts  27.6 us (9%)
  other arithmetic  15.7 us (5%)
    pallas_call x4, Pallas kernels, shift_sum(): pl.pallas_call(functools.partial(shift_sum_kernel, int(has_base)), out_sh...  66.2 us
    ppermute x6, waiting for transfers between devices, from_partner(): lax.ppermute(value, axis, [(i, i ^ 1 << stride) for i in range(lax.axis_s...  55.8 us
    all_to_all x4, waiting for transfers between devices, per_device(): lax.all_to_all(chunk, 'freq', split_axis=0, concat_axis=0, tiled=True)  36.7 us
    all_to_all x1, waiting for transfers between devices, per_device(): lax.all_to_all(slabs, 'freq', split_axis=0, concat_axis=0, tiled=True)  22.3 us
    all_to_all x4, starting transfers between devices, per_device(): lax.all_to_all(chunk, 'freq', split_axis=0, concat_axis=0, tiled=True)  20.6 us
    pallas_call x1, Pallas kernels, template_search(): pl.pallas_call(template_kernel, out_shape=jax.ShapeDtypeStruct((rows, bin...  19.1 us
    unnamed x31, local copies, waits for them, and re-layouts  16.7 us
    pallas_call x1, Pallas kernels, dft(): pl.pallas_call(dft_kernel, out_shape=jax.ShapeDtypeStruct((slabs, 2, row_...  12.1 us
  transfers between devices with their start and end apart: 13, of which 10 were waited for; matrix products, arithmetic and copies ran while one was open for 4% of the time, Pallas kernels for 19%

profile of v1, /device:TPU:0, one launch (start us, length us, event | category | flops | bytes accessed | tf_op | source)
XLA Modules:
  0.0 299.1 jit_solution(13299946246251410449)
XLA Ops:
  0.0 2.8 slice.110
  2.8 7.3 %all-to-all-start.1 = ((f32[8,24,2048]{2,1,0:T(8,128)}), f32[8,24,2048]{2,1,0:T(8,128)S(1)}, u32[]{:S(2)}, u32[]{:S(2)}) async-start(f32[8,24,2048]{2,1,0:T(8,128)} %slice.110), calls=%async_computation.1 | async-start | bytes 3145728 | tf_op jit(solution)/shard_map/all_to_all | solution.py:284
  10.1 3.1 %fusion.28 = (f32[8,16,2048]{2,1,0:T(8,128)}, f32[8,16,2048]{2,1,0:T(8,128)}) fusion(f32[8,64,2048]{2,1,0:T(8,128)} %bitcast.35), kind=kLoop, calls=%fused_computation.101 | loop fusion | bytes 4194304 | tf_op jit(solution)/shard_map/slice | solution.py:281
  13.2 33.9 %all-to-all-done.1.series_ref = f32[8,24,2048]{2,1,0:T(8,128)S(1)} async-done(((f32[8,24,2048]{2,1,0:T(8,128)}), f32[8,24,2048]{2,1,0:T(8,128)S(1)}, u32[]{:S(2)}, u32[]{:S(2)}) %all-to-all-start.1) | async-done | bytes 1572896 | tf_op jit(solution)/shard_map/all_to_all | solution.py:284
  48.3 3.6 %all-to-all-start = ((f32[8,16,2048]{2,1,0:T(8,128)}), f32[8,16,2048]{2,1,0:T(8,128)S(1)}, u32[]{:S(2)}, u32[]{:S(2)}) async-start(f32[8,16,2048]{2,1,0:T(8,128)} %get-tuple-element.15), calls=%async_computation | async-start | bytes 2097152 | tf_op jit(solution)/shard_map/all_to_all | solution.py:284
  53.5 24.0 %shift_sum.4.refs_0_ = f32[64,128,128]{2,1,0:T(8,128)S(1)} custom-call(s32[24,64]{1,0:T(8,128)S(1)} %copy.24.delay_ref, f32[8,24,2048]{2,1,0:T(8,128)S(1)} %copy-done.7), custom_call_target="tpu_custom_call" | custom-call | flops 3145728000 | bytes 5767168 | tf_op jit(solution)/shard_map/shift_sum/pallas_call | solution.py:105
  79.4 6.0 %all-to-all-start.3 = ((f32[8,16,2048]{2,1,0:T(8,128)}), f32[8,16,2048]{2,1,0:T(8,128)S(1)}, u32[]{:S(2)}, u32[]{:S(2)}) async-start(f32[8,16,2048]{2,1,0:T(8,128)} %get-tuple-element.8), calls=%async_computation.3 | async-start | bytes 2097152 | tf_op jit(solution)/shard_map/all_to_all | solution.py:284
  89.7 16.6 %shift_sum.5.refs_0_ = f32[64,128,128]{2,1,0:T(8,128)S(1)} custom-call(s32[16,64]{1,0:T(8,128)S(1)} %copy.23.delay_ref, f32[8,16,2048]{2,1,0:T(8,128)S(1)} %all-to-all-done.series_ref, f32[64,128,128]{2,1,0:T(8,128)S(1)} %copy-done.1), custom_call_target="tpu_custom_call", output_to_operand_aliasing={{}: (2, {})} | custom-call | flops 2097152000 | bytes 5242880 | tf_op jit(solution)/shard_map/shift_sum/pallas_call | solution.py:105
  108.2 2.8 all-to-all-done.3.series_ref
  111.0 3.7 %all-to-all-start.2 = ((f32[8,8,2048]{2,1,0:T(8,128)}), f32[8,8,2048]{2,1,0:T(8,128)S(1)}, u32[]{:S(2)}, u32[]{:S(2)}) async-start(f32[8,8,2048]{2,1,0:T(8,128)} %slice.108), calls=%async_computation.2 | async-start | bytes 1048576 | tf_op jit(solution)/shard_map/all_to_all | solution.py:284
  117.1 16.6 %shift_sum.6.refs_0_ = f32[64,128,128]{2,1,0:T(8,128)S(1)} custom-call(s32[16,64]{1,0:T(8,128)S(1)} %copy.25.delay_ref, f32[8,16,2048]{2,1,0:T(8,128)S(1)} %all-to-all-done.3.series_ref, f32[64,128,128]{2,1,0:T(8,128)S(1)} %copy-done.3), custom_call_target="tpu_custom_call", output_to_operand_aliasing={{}: (2, {})} | custom-call | flops 2097152000 | bytes 5242880 | tf_op jit(solution)/shard_map/shift_sum/pallas_call | solution.py:105
  137.8 9.1 %shift_sum.7 = f32[64,128,128]{2,1,0:T(8,128)S(1)} custom-call(s32[8,64]{1,0:T(8,128)S(1)} %copy.22.delay_ref, f32[8,8,2048]{2,1,0:T(8,128)S(1)} %all-to-all-done.2.series_ref, f32[64,128,128]{2,1,0:T(8,128)S(1)} %copy-done.5), custom_call_target="tpu_custom_call", output_to_operand_aliasing={{}: (2, {})} | custom-call | flops 1048576000 | bytes 4718592 | tf_op jit(solution)/shard_map/shift_sum/pallas_call | solution.py:105
  152.9 20.4 %collective-permute-done = f32[2,8,128,128]{3,2,1,0:T(8,128)} collective-permute-done((f32[2,8,128,128]{3,2,1,0:T(8,128)S(1)}, f32[2,8,128,128]{3,2,1,0:T(8,128)}, u32[]{:S(2)}, u32[]{:S(2)}) %collective-permute-start) | collective-permute-done | bytes 1048608 | tf_op jit(solution)/shard_map/ppermute | solution.py:22
  179.8 7.7 %collective-permute-done.1 = f32[8,128,128]{2,1,0:T(8,128)S(1)} collective-permute-done((f32[8,128,128]{2,1,0:T(8,128)S(1)}, f32[8,128,128]{2,1,0:T(8,128)S(1)}, u32[]{:S(2)}, u32[]{:S(2)}) %collective-permute-start.1) | collective-permute-done | bytes 524320 | tf_op jit(solution)/shard_map/ppermute | solution.py:22
  187.6 2.8 collective-permute-done.3
  191.5 12.1 %dft.1 = f32[8,2,16,8,128]{4,3,2,1,0:T(8,128)} custom-call(bf16[384,256]{1,0:T(8,128)(2,1)} %constant.175.clone.first_ref, f32[128,128]{1,0:T(8,128)} %constant.177.clone.twist_cos_ref, f32[128,128]{1,0:T(8,128)} %constant.178.clone.twist_sin_ref, bf16[128,768]{1,0:T(8,128)(2,1)} %constant.176.clone.second_ref, f32[16,128,128]{2,1,0:T(8,128)} %pad_maximum_fusion.series_ref), custom_call_target="tpu_custom_call" | custom-call | tf_op jit(solution)/shard_map/dft/pallas_call | solution.py:201
  203.6 4.6 %all-to-all-start.4 = ((f32[8,2,16,8,128]{4,3,2,1,0:T(8,128)}), f32[8,2,16,8,128]{4,3,2,1,0:T(8,128)S(1)}, u32[]{:S(2)}, u32[]{:S(2)}) async-start(f32[8,2,16,8,128]{4,3,2,1,0:T(8,128)} %dft.1), calls=%async_computation.4 | async-start | bytes 2097152 | tf_op jit(solution)/shard_map/all_to_all | solution.py:302
  209.5 22.3 %all-to-all-done.4 = f32[8,2,16,8,128]{4,3,2,1,0:T(8,128)S(1)} async-done(((f32[8,2,16,8,128]{4,3,2,1,0:T(8,128)}), f32[8,2,16,8,128]{4,3,2,1,0:T(8,128)S(1)}, u32[]{:S(2)}, u32[]{:S(2)}) %all-to-all-start.4) | async-done | bytes 1048608 | tf_op jit(solution)/shard_map/all_to_all | solution.py:302
  232.1 2.8 fusion.11
  238.1 2.6 slice_add_fusion.3
  243.2 22.8 %collective-permute-done.5 = f32[2,1,128,1024]{3,2,1,0:T(8,128)S(1)} collective-permute-done((f32[2,1,128,1024]{3,2,1,0:T(8,128)S(1)}, f32[2,1,128,1024]{3,2,1,0:T(8,128)S(1)}, u32[]{:S(2)}, u32[]{:S(2)}) %collective-permute-start.5) | collective-permute-done | bytes 1048608 | tf_op jit(solution)/shard_map/ppermute | solution.py:22
  269.1 3.1 %collective-permute-start.6 = (f32[2,128,32]{2,1,0:T(8,128)S(1)}, f32[2,128,32]{2,1,0:T(8,128)S(1)}, u32[]{:S(2)}, u32[]{:S(2)}) collective-permute-start(f32[2,128,32]{2,1,0:T(8,128)S(1)} %get-tuple-element.27), channel_id=1, source_target_pairs={{0,1},{1,2},{2,3},{3,4},{4,5},{5,6},{6,7},{8,9},{9,10},{10,11},{11... | collective-permute-start | bytes 98312 | tf_op jit(solution)/shard_map/ppermute | solution.py:33
  274.7 4.4 %collective-permute-done.7 = f32[2,128,32]{2,1,0:T(8,128)S(1)} collective-permute-done((f32[2,128,32]{2,1,0:T(8,128)S(1)}, f32[2,128,32]{2,1,0:T(8,128)S(1)}, u32[]{:S(2)}, u32[]{:S(2)}) %collective-permute-start.7) | collective-permute-done | bytes 32800 | tf_op jit(solution)/shard_map/ppermute | solution.py:35
  279.9 19.1 %template_search.1 = f32[128,1024]{1,0:T(8,128)} custom-call(f32[32,256]{1,0:T(8,128)S(1)} %select_reduce_fusion.profile_ref, f32[256,1152]{1,0:T(8,128)S(1)} %bitcast.28, f32[256,1152]{1,0:T(8,128)S(1)} %bitcast.29), custom_call_target="tpu_custom_call" | custom-call | tf_op jit(solution)/shard_map/template_search/pallas_call | solution.py:245
  (77 shorter events, 44.7 us)
Async XLA Ops:
  2.8 44.3 %all-to-all-start.1 = ((f32[8,24,2048]{2,1,0:T(8,128)}), f32[8,24,2048]{2,1,0:T(8,128)S(1)}, u32[]{:S(2)}, u32[]{:S(2)}) async-start(f32[8,24,2048]{2,1,0:T(8,128)} %slice.110), calls=%async_computation.1 | async-start | bytes 3145728 | tf_op jit(solution)/shard_map/all_to_all | solution.py:284
  13.2 38.7 %copy-start.9 = (s32[512,64]{0,1:T(8,128)S(1)}, s32[512,64]{0,1:T(8,128)}, u32[]{:S(2)}) copy-start(s32[512,64]{0,1:T(8,128)} %param.10) | copy-start | bytes 393220
  48.3 31.2 %all-to-all-start = ((f32[8,16,2048]{2,1,0:T(8,128)}), f32[8,16,2048]{2,1,0:T(8,128)S(1)}, u32[]{:S(2)}, u32[]{:S(2)}) async-start(f32[8,16,2048]{2,1,0:T(8,128)} %get-tuple-element.15), calls=%async_computation | async-start | bytes 2097152 | tf_op jit(solution)/shard_map/all_to_all | solution.py:284
  52.1 1.4 copy-start.7
  77.5 2.0 copy-start
  79.4 31.6 %all-to-all-start.3 = ((f32[8,16,2048]{2,1,0:T(8,128)}), f32[8,16,2048]{2,1,0:T(8,128)S(1)}, u32[]{:S(2)}, u32[]{:S(2)}) async-start(f32[8,16,2048]{2,1,0:T(8,128)} %get-tuple-element.8), calls=%async_computation.3 | async-start | bytes 2097152 | tf_op jit(solution)/shard_map/all_to_all | solution.py:284
  87.5 2.2 copy-start.1
  106.3 2.0 copy-start.2
  111.0 24.6 %all-to-all-start.2 = ((f32[8,8,2048]{2,1,0:T(8,128)}), f32[8,8,2048]{2,1,0:T(8,128)S(1)}, u32[]{:S(2)}, u32[]{:S(2)}) async-start(f32[8,8,2048]{2,1,0:T(8,128)} %slice.108), calls=%async_computation.2 | async-start | bytes 1048576 | tf_op jit(solution)/shard_map/all_to_all | solution.py:284
  114.9 2.2 copy-start.3
  133.7 2.0 copy-start.4
  135.6 2.2 copy-start.5
  148.6 24.7 %collective-permute-start = (f32[2,8,128,128]{3,2,1,0:T(8,128)S(1)}, f32[2,8,128,128]{3,2,1,0:T(8,128)}, u32[]{:S(2)}, u32[]{:S(2)}) collective-permute-start(f32[2,8,128,128]{3,2,1,0:T(8,128)S(1)} %dynamic-slice_bitcast_fusion.1), channel_id=1, source_target_pairs={{0,1},{1,0},{2,3},{3,2},{4,5},{5,4},{6,7},{7,6},{8,9},{9,8},{10,11... | collective-permute-start | bytes 3145736 | tf_op jit(solution)/shard_map/ppermute | solution.py:22
  151.5 25.3 %collective-permute-start.2 = (f32[2,8,128,128]{3,2,1,0:T(8,128)}, f32[2,8,128,128]{3,2,1,0:T(8,128)}, u32[]{:S(2)}, u32[]{:S(2)}) collective-permute-start(f32[2,8,128,128]{3,2,1,0:T(8,128)} %dynamic-slice_bitcast_fusion), channel_id=1, source_target_pairs={{0,2},{1,3},{2,0},{3,1},{4,6},{5,7},{6,4},{7,5},{8,10},{9,11},{10,... | collective-permute-start | bytes 3145736 | tf_op jit(solution)/shard_map/ppermute | solution.py:22
  175.0 12.5 %collective-permute-start.1 = (f32[8,128,128]{2,1,0:T(8,128)S(1)}, f32[8,128,128]{2,1,0:T(8,128)S(1)}, u32[]{:S(2)}, u32[]{:S(2)}) collective-permute-start(f32[8,128,128]{2,1,0:T(8,128)S(1)} %dynamic-slice_bitcast_fusion.3), channel_id=1, source_target_pairs={{0,2},{1,3},{2,0},{3,1},{4,6},{5,7},{6,4},{7,5},{8,10},{9,11},{10,... | collective-permute-start | bytes 1572872 | tf_op jit(solution)/shard_map/ppermute | solution.py:22
  178.2 12.2 %collective-permute-start.3 = (f32[8,128,128]{2,1,0:T(8,128)S(1)}, f32[8,128,128]{2,1,0:T(8,128)S(1)}, u32[]{:S(2)}, u32[]{:S(2)}) collective-permute-start(f32[8,128,128]{2,1,0:T(8,128)S(1)} %dynamic-slice_bitcast_fusion.2), channel_id=1, source_target_pairs={{0,1},{1,0},{2,3},{3,2},{4,5},{5,4},{6,7},{7,6},{8,9},{9,8},{10,11... | collective-permute-start | bytes 1572872 | tf_op jit(solution)/shard_map/ppermute | solution.py:22
  191.5 16.7 %copy-start.12 = (s32[7]{0:T(128)S(1)}, s32[7]{0:T(128)}, u32[]{:S(2)}) copy-start(s32[7]{0:T(128)} %param.11) | copy-start | bytes 88
  203.6 28.2 %all-to-all-start.4 = ((f32[8,2,16,8,128]{4,3,2,1,0:T(8,128)}), f32[8,2,16,8,128]{4,3,2,1,0:T(8,128)S(1)}, u32[]{:S(2)}, u32[]{:S(2)}) async-start(f32[8,2,16,8,128]{4,3,2,1,0:T(8,128)} %dft.1), calls=%async_computation.4 | async-start | bytes 2097152 | tf_op jit(solution)/shard_map/all_to_all | solution.py:302
  235.1 2.7 collective-permute-start.4
  238.0 4.3 %copy-start.11 = (s32[32,16]{0,1:T(8,128)S(1)}, s32[32,16]{0,1:T(8,128)}, u32[]{:S(2)}) copy-start(s32[32,16]{0,1:T(8,128)} %param.12) | copy-start | bytes 6148
  238.0 4.4 %copy-start.10 = (f32[32,16]{0,1:T(8,128)S(1)}, f32[32,16]{0,1:T(8,128)}, u32[]{:S(2)}) copy-start(f32[32,16]{0,1:T(8,128)} %param.13) | copy-start | bytes 6148
  240.8 25.3 %collective-permute-start.5 = (f32[2,1,128,1024]{3,2,1,0:T(8,128)S(1)}, f32[2,1,128,1024]{3,2,1,0:T(8,128)S(1)}, u32[]{:S(2)}, u32[]{:S(2)}) collective-permute-start(f32[2,1,128,1024]{3,2,1,0:T(8,128)S(1)} %maximum_multiply_fusion.1), channel_id=1, source_target_pairs={{0,16},{8,24},{16,0},{24,8},{1,17},{9,25},{17,1},{25,9},{2,18},{10... | collective-permute-start | bytes 3145736 | tf_op jit(solution)/shard_map/ppermute | solution.py:22
  269.1 5.6 %collective-permute-start.6 = (f32[2,128,32]{2,1,0:T(8,128)S(1)}, f32[2,128,32]{2,1,0:T(8,128)S(1)}, u32[]{:S(2)}, u32[]{:S(2)}) collective-permute-start(f32[2,128,32]{2,1,0:T(8,128)S(1)} %get-tuple-element.27), channel_id=1, source_target_pairs={{0,1},{1,2},{2,3},{3,4},{4,5},{5,6},{6,7},{8,9},{9,10},{10,11},{11... | collective-permute-start | bytes 98312 | tf_op jit(solution)/shard_map/ppermute | solution.py:33
  272.2 6.9 %collective-permute-start.7 = (f32[2,128,32]{2,1,0:T(8,128)S(1)}, f32[2,128,32]{2,1,0:T(8,128)S(1)}, u32[]{:S(2)}, u32[]{:S(2)}) collective-permute-start(f32[2,128,32]{2,1,0:T(8,128)S(1)} %get-tuple-element.26), channel_id=1, source_target_pairs={{1,0},{2,1},{3,2},{4,3},{5,4},{6,5},{7,6},{9,8},{10,9},{11,10},{12... | collective-permute-start | bytes 98312 | tf_op jit(solution)/shard_map/ppermute | solution.py:35
  (2 other events, 2.6 us)

commit v2 on v1

--- a/solution.py
+++ b/solution.py
@@ -22,23 +22,6 @@
     return lax.ppermute(value, axis, [(i, i ^ 1 << stride) for i in range(lax.axis_size(axis))])
 
 
-def extended(cells, sides, width):
-    for axis, dim in sides:
-        count = lax.axis_size(axis)
-        ends = count - 1
-        head = lax.slice_in_dim(cells, 0, width, axis=dim)
-        tail = lax.slice_in_dim(cells, cells.shape[dim] - width, cells.shape[dim], axis=dim)
-        cells = jnp.concatenate(
-            [
-                lax.ppermute(tail, axis, [(i, (i + 1) % count) for i in range(ends)]),
-                cells,
-                lax.ppermute(head, axis, [((i + 1) % count, i) for i in range(ends)]),
-            ],
-            axis=dim,
-        )
-    return cells
-
-
 def turning(count, modulus):
     angle = (count % modulus).astype(jnp.float32) * (two_pi / modulus)
     return (jnp.cos(angle), jnp.sin(angle))
@@ -48,9 +31,9 @@
     return (real * cosine + imag * sine_part, imag * cosine - real * sine_part)
 
 
-def merge_nodes(lower_half, upper_half, out_index, slopes, bins_index, modulus):
-    shift = out_index[None, :] * slopes[:, None] // 16 % modulus
-    cosine, sine_part = turning(shift[:, :, None] * bins_index[None, None, :], modulus)
+def merge_nodes(lower_half, upper_half, out_index, slope, bins_index, modulus):
+    shift = out_index * slope // 16 % modulus
+    cosine, sine_part = turning(shift[None, :, None] * bins_index[:, None, :], modulus)
     up_re, up_im = rotate(upper_half[0], upper_half[1], cosine, sine_part)
     return jnp.stack([lower_half[0] + up_re, lower_half[1] + up_im]) * (1.0 / math.sqrt(2.0))
 
@@ -129,9 +112,9 @@
 
 def chunk_sizes(group_count):
     if group_count < 8:
-        return [1] * group_count if group_count <= 4 else [group_count - 3, 1, 1, 1]
+        return [1] * group_count
     last = group_count // 8
-    return [group_count - 5 * last, 2 * last, 2 * last, last]
+    return [group_count - 4 * last, 3 * last, last]
 
 
 def reduce_halving(value, pos, bits):
@@ -159,34 +142,50 @@
 
 
 def dft_kernel(first_ref, twist_cos_ref, twist_sin_ref, second_ref, series_ref, out_ref):
-    count = series_ref.shape[2]
-    coarse, fine = split_halves(series_ref[0])
+    rows, inner, outer = series_ref.shape
+    coarse, fine = split_halves(series_ref[...].reshape(rows * inner, outer))
     part_out = jnp.dot(
         jnp.concatenate([coarse, fine, coarse], axis=1),
         first_ref[...],
         preferred_element_type=jnp.float32,
     )
-    real, imag = rotate(
-        part_out[:, :count], part_out[:, count:], twist_cos_ref[...], twist_sin_ref[...]
-    )
-    coarse, fine = split_halves(jnp.concatenate([real, imag], axis=0))
+    turned = []
+    for row in range(rows):
+        part = part_out[row * inner : (row + 1) * inner]
+        real, imag = rotate(
+            part[:, :outer], part[:, outer:], twist_cos_ref[...], twist_sin_ref[...]
+        )
+        turned.append(jnp.concatenate([real, imag], axis=0))
+    coarse, fine = split_halves(jnp.concatenate(turned, axis=1))
     spectrum = jnp.dot(
         second_ref[...],
         jnp.concatenate([coarse, fine, coarse], axis=0),
         preferred_element_type=jnp.float32,
     )
-    slabs, _, _, rows, _ = out_ref.shape
-    half = slabs * rows
-    for slab in range(slabs):
-        out_ref[slab, 0, 0] = spectrum[slab * rows : (slab + 1) * rows]
-        out_ref[slab, 1, 0] = spectrum[half + slab * rows : half + (slab + 1) * rows]
+    slabs, _, tiles, _, _ = out_ref.shape
+    tiles -= 1
+    half = slabs * tiles
+    lane = lax.broadcasted_iota(jnp.int32, (1, outer), 1)
+    none = jnp.zeros((1, outer), jnp.float32)
+    for row in range(rows):
+        for part in range(2):
+            bins = spectrum[part * half : (part + 1) * half, row * outer : (row + 1) * outer]
+            for slab in range(slabs):
+                low, high = slab * tiles, (slab + 1) * tiles
+                out_ref[slab, part, 0:tiles, row, :] = bins[low:high]
+                after = bins[high : high + 1] if high < half else none
+                before = bins[low - 1 : low] if low else none
+                out_ref[slab, part, tiles, row : row + 1, :] = jnp.where(
+                    lane < outer // 2, after, before
+                )
 
 
 def dft(series, slabs, scale):
     row_count, inner, outer = series.shape
     length = inner * outer
     kept = inner // 2
-    rows = kept // slabs
+    tiles = kept // slabs + 1
+    rows = math.gcd(row_count, 8)
     index = np.arange(outer)
     angle = (index[:, None] * index[None, :] % outer) * (two_pi / outer)
     first = np.concatenate([np.cos(angle), -np.sin(angle)], axis=1)
@@ -200,16 +199,16 @@
     whole = [pl.BlockSpec(t.shape, lambda i: (0, 0)) for t in tables]
     return pl.pallas_call(
         dft_kernel,
-        out_shape=jax.ShapeDtypeStruct((slabs, 2, row_count, rows, outer), jnp.float32),
-        grid=(row_count,),
-        in_specs=whole
-        + [pl.BlockSpec((1, inner, outer), lambda i: (i, 0, 0))],
-        out_specs=pl.BlockSpec((slabs, 2, 1, rows, outer), lambda i: (0, 0, i, 0, 0)),
+        out_shape=jax.ShapeDtypeStruct((slabs, 2, tiles, row_count, outer), jnp.float32),
+        grid=(row_count // rows,),
+        in_specs=whole + [pl.BlockSpec((rows, inner, outer), lambda i: (i, 0, 0))],
+        out_specs=pl.BlockSpec((slabs, 2, tiles, rows, outer), lambda i: (0, 0, 0, i, 0)),
         name="dft",
     )(*tables, series)
 
 
-def template_kernel(profile_ref, left_ref, right_ref, out_ref, bank_ref):
+def template_kernel(first_step, profile_ref, before_ref, tile_ref, after_ref, *refs):
+    out_ref, bank_ref = refs[-2:]
     template_count, width = profile_ref.shape
 
     @pl.when(pl.program_id(0) == 0)
@@ -223,9 +222,14 @@
 
         lax.fori_loop(0, template_count, one_template, 0)
 
-    coarse, fine = split_halves(jnp.concatenate([left_ref[...], right_ref[...]], axis=1))
+    rows = out_ref.shape[0]
+    lane = lax.broadcasted_iota(jnp.int32, (2 * rows, LANES), 1)
+    tile, after, before = (
+        ref[...].reshape(2 * rows, LANES) for ref in (tile_ref, after_ref, before_ref)
+    )
+    border = jnp.where(lane < LANES // 2, after, before)
+    coarse, fine = split_halves(jnp.concatenate([tile, border], axis=1))
     cells = jnp.concatenate([coarse, fine, coarse], axis=1)
-    rows = out_ref.shape[0]
     best = jnp.zeros_like(out_ref)
     for pair in range(template_count // 2):
         corr = lax.dot_general(
@@ -239,23 +243,34 @@
     out_ref[...] = best
 
 
-def template_search(profile, cells, bins_dev):
-    rows = cells.shape[0] // 2
+def template_search(profile, cells, borders, tiles, first, filled):
+    run, rows = cells.shape[1:3]
     template_count, width = profile.shape
+    shape = (2, 1, rows, LANES)
+    cells = jnp.concatenate([borders[:, :1], cells, borders[:, 1:]], axis=1)
+    specs = [pl.BlockSpec((template_count, width), lambda i: (0, 0))]
+    for step in range(3):
+        specs.append(pl.BlockSpec(shape, lambda i, step=step: (0, i + step, 0, 0)))
+    operands = [profile, cells, cells, cells]
+    if filled is not None:
+        specs.append(pl.BlockSpec(memory_space=pl.ANY))
+        operands.append(filled)
     return pl.pallas_call(
-        template_kernel,
-        out_shape=jax.ShapeDtypeStruct((rows, bins_dev), jnp.float32),
-        grid=(bins_dev // LANES,),
-        in_specs=[
-            pl.BlockSpec((template_count, width), lambda i: (0, 0)),
-            pl.BlockSpec((2 * rows, LANES), lambda i: (0, i)),
-            pl.BlockSpec((2 * rows, LANES), lambda i: (0, i + 1)),
-        ],
-        out_specs=pl.BlockSpec((rows, LANES), lambda i: (0, i)),
+        functools.partial(template_kernel, first),
+        out_shape=jax.ShapeDtypeStruct((rows, tiles * LANES), jnp.float32),
+        grid=(run,),
+        in_specs=specs,
+        out_specs=pl.BlockSpec((rows, LANES), lambda i: (0, i + first)),
         scratch_shapes=[pltpu.VMEM((template_count * LANES, 3 * width), jnp.bfloat16)],
+        input_output_aliases={} if filled is None else {4: 0},
+        cost_estimate=pl.CostEstimate(
+            flops=1000 * run * rows * template_count * width * LANES,
+            bytes_accessed=4 * cells.size,
+            transcendentals=0,
+        ),
         compiler_params=pltpu.CompilerParams(vmem_limit_bytes=48 << 20),
         name="template_search",
-    )(profile, cells, cells)
+    )(*operands)
 
 
 def per_device(samples, channel_delay, merge_slope, tap_offset, tap_weight):
@@ -271,8 +286,6 @@
     per_sub = chan_dev // 2
     chan_own = chan_dev // freq_count
     share = per_sub // chan_own
-    bins_index = freq_pos * bins_dev + lax.iota(jnp.int32, bins_dev)
-
     own_delay = lax.dynamic_slice_in_dim(channel_delay, freq_pos * chan_own, chan_own, axis=0)
     by_owner = samples.reshape(freq_count, chan_own, samp_dev)
     start, waiting, previous, partial = 0, None, None, None
@@ -300,41 +313,64 @@
     )
     slabs = dft(owned, freq_count, 1.0 / math.sqrt(length * per_sub))
     slabs = lax.all_to_all(slabs, "freq", split_axis=0, concat_axis=0, tiled=True)
+    tiles = bins_dev // LANES
+    spot = lax.iota(jnp.int32, bins_dev + LANES)
+    spot = jnp.where(spot < bins_dev + LANES // 2, spot, spot - bins_dev - LANES)
+    bins_index = (freq_pos * bins_dev + spot).reshape(tiles + 1, LANES)
     subband_sums = (
-        slabs.reshape(2, share, 2, 2, rows, bins_dev)
-        .transpose(2, 0, 3, 1, 4, 5)
-        .reshape(2, 2, delays_sub, bins_dev)
-    )
-    lower_half = jnp.concatenate([subband_sums[:, 0:1], subband_sums[:, 0:1]], axis=2)
-    upper_half = jnp.concatenate([subband_sums[:, 1:2], subband_sums[:, 1:2]], axis=2)
-    first_slope = pick_entry(merge_slope, 2 * band_pos).reshape(1)
-    level_zero = merge_nodes(
-        lower_half, upper_half, lax.iota(jnp.int32, block_rows), first_slope, bins_index, length
-    )
-    section_count = band_count.bit_length() - 1
-    current = level_zero
-    for section_no in range(1, section_count + 1):
+        slabs.reshape(2, share, 2, tiles + 1, 2, rows, LANES)
+        .transpose(2, 0, 3, 4, 1, 5, 6)
+        .reshape(2, 2, tiles + 1, delays_sub, LANES)
+    )
+    first_slope = pick_entry(merge_slope, 2 * band_pos)
+    current = merge_nodes(
+        jnp.concatenate([subband_sums[:, 0]] * 2, axis=2),
+        jnp.concatenate([subband_sums[:, 1]] * 2, axis=2),
+        lax.iota(jnp.int32, block_rows), first_slope, bins_index, length,
+    )
+
+    def section(current, partner, section_no, bins_index):
         group_size = 1 << section_no
-        half_size = group_size >> 1
         position = band_pos % group_size
-        partner = from_partner(current, "band", section_no - 1)
-        upper_side = position >= half_size
+        upper_side = position >= group_size >> 1
         lower_half = jnp.where(upper_side, partner, current)
         upper_half = jnp.where(upper_side, current, partner)
         node_no = band_pos // group_size
-        section_slope = pick_entry(
-            merge_slope, node_no * (2 * group_size) + group_size - 1
-        ).reshape(1)
+        slope = pick_entry(merge_slope, node_no * (2 * group_size) + group_size - 1)
         out_index = position * block_rows + lax.iota(jnp.int32, block_rows)
-        current = merge_nodes(lower_half, upper_half, out_index, section_slope, bins_index, length)
-    spectra = current[:, 0]
-    bordered = extended(spectra, (("freq", 2),), REACH)
+        return merge_nodes(lower_half, upper_half, out_index, slope, bins_index, length)
+
+    section_count = band_count.bit_length() - 1
+    for section_no in range(1, section_count):
+        partner = from_partner(current, "band", section_no - 1)
+        current = section(current, partner, section_no, bins_index)
+
     width = 2 * LANES
     span = lax.iota(jnp.int32, width)
-    matches = tap_offset[:, :, None] + REACH == span[None, None, :]
+    matches = (tap_offset % width)[:, :, None] == span[None, None, :]
     profile = jnp.sum(jnp.where(matches, tap_weight[:, :, None], 0.0), axis=1)
-    cells = jnp.pad(bordered, ((0, 0), (0, 0), (0, LANES - 2 * REACH)))
-    return template_search(profile, cells.reshape(2 * block_rows, bins_dev + LANES), bins_dev)
+
+    cut = tiles // 2
+    early = jnp.concatenate([current[:, tiles:], current[:, : cut + 1]], axis=1)
+    early_bins = jnp.concatenate([bins_index[tiles:], bins_index[: cut + 1]])
+    late, late_bins = current[:, cut + 1 : tiles], bins_index[cut + 1 : tiles]
+    if section_count:
+        early_partner = from_partner(early, "band", section_count - 1)
+        early_partner, late = lax.optimization_barrier((early_partner, late))
+        late_partner = from_partner(late, "band", section_count - 1)
+        early = section(early, early_partner, section_count, early_bins)
+    power = template_search(
+        profile, early[:, 1 : cut + 1], early[:, :: cut + 1], tiles, 0, None
+    )
+    if section_count:
+        late, power = lax.optimization_barrier((late, power))
+        late = section(late, late_partner, section_count, late_bins)
+    return template_search(
+        profile,
+        jnp.concatenate([early[:, cut + 1 :], late], axis=1),
+        jnp.concatenate([early[:, cut : cut + 1], early[:, :1]], axis=1),
+        tiles, cut, power,
+    )
 
 
 def solution(mesh):

time: 301 us -> 286 us (0.950)
  local copies, waits for them, and re-layouts: 27.6 us -> 19.7 us
  starting transfers between devices: 37.9 us -> 31 us
  other arithmetic: 15.7 us -> 20.4 us
    all_to_all x4 -> x3, waiting for transfers between devices: 36.7 us -> 46.5 us  [per_device(): lax.all_to_all(chunk, 'freq', split_axis=0, concat_axis=0, tiled=True)]
    ppermute x6 -> x7, waiting for transfers between devices: 55.8 us -> 47 us  [from_partner(): lax.ppermute(value, axis, [(i, i ^ 1 << stride) for i in range(lax.axis_s...]
    unnamed x31 -> x32, local copies, waits for them, and re-layouts: 16.7 us -> 8.12 us
    ppermute x2 -> x0, waiting for transfers between devices: 5.3 us -> none  [the longest x1 4.36 us: extended(): lax.ppermute(head, axis, [((i + 1) % count, i) for i in range(ends)])]
    ppermute x2 -> x0, starting transfers between devices: 4.4 us -> none  [the longest x1 3.11 us: extended(): lax.ppermute(tail, axis, [(i, (i + 1) % count) for i in range(ends)])]
    all_to_all x4 -> x3, starting transfers between devices: 20.6 us -> 16.6 us  [per_device(): lax.all_to_all(chunk, 'freq', split_axis=0, concat_axis=0, tiled=True)]
    pallas_call x2 -> x3, Pallas kernels: 31.2 us -> 27.7 us  [the longest x2 23.4 us: template_search(): pl.pallas_call(functools.partial(template_kernel, first), out_shape=jax.S...]
    add x2 -> x4, other arithmetic: 5.34 us -> 8.6 us  [merge_nodes(): lower_half[0] + up_re]
  transfers between devices with their start and end apart: 13 -> 11, of which waited for: 10 -> 8; matrix products, arithmetic and copies ran while one was open for 4% -> 5% of each run, Pallas kernels for 19% -> 25%
where the time goes in v2:
time: 286 us; the launch traced here: 285 us
  waiting for transfers between devices  117 us (41%)
  Pallas kernels  95.6 us (33%)
  starting transfers between devices  31 us (11%)
  other arithmetic  20.4 us (7%)
  local copies, waits for them, and re-layouts  19.7 us (7%)
    pallas_call x3, Pallas kernels, shift_sum(): pl.pallas_call(functools.partial(shift_sum_kernel, int(has_base)), out_sh...  67.9 us
    ppermute x7, waiting for transfers between devices, from_partner(): lax.ppermute(value, axis, [(i, i ^ 1 << stride) for i in range(lax.axis_s...  47 us
    all_to_all x3, waiting for transfers between devices, per_device(): lax.all_to_all(chunk, 'freq', split_axis=0, concat_axis=0, tiled=True)  46.5 us
    all_to_all x1, waiting for transfers between devices, per_device(): lax.all_to_all(slabs, 'freq', split_axis=0, concat_axis=0, tiled=True)  23.9 us
    pallas_call x2, Pallas kernels, template_search(): pl.pallas_call(functools.partial(template_kernel, first), out_shape=jax.S...  23.4 us
    all_to_all x3, starting transfers between devices, per_device(): lax.all_to_all(chunk, 'freq', split_axis=0, concat_axis=0, tiled=True)  16.6 us
    ppermute x7, starting transfers between devices, from_partner(): lax.ppermute(value, axis, [(i, i ^ 1 << stride) for i in range(lax.axis_s...  9.7 us
    add x4, other arithmetic, merge_nodes(): lower_half[0] + up_re  8.6 us
  transfers between devices with their start and end apart: 11, of which 8 were waited for; matrix products, arithmetic and copies ran while one was open for 5% of the time, Pallas kernels for 25%

profile of v2, /device:TPU:0, one launch (start us, length us, event | category | flops | bytes accessed | tf_op | source)
XLA Modules:
  0.0 284.7 jit_solution(9406636888051386868)
XLA Ops:
  0.0 3.2 %slice.165 = f32[8,32,2048]{2,1,0:T(8,128)} slice(f32[8,64,2048]{2,1,0:T(8,128)} %bitcast.37), slice={[0:8], [0:32], [0:2048]} | slice | bytes 4194304 | tf_op jit(solution)/shard_map/slice | solution.py:294
  3.2 7.3 %all-to-all-start = ((f32[8,32,2048]{2,1,0:T(8,128)}), f32[8,32,2048]{2,1,0:T(8,128)S(1)}, u32[]{:S(2)}, u32[]{:S(2)}) async-start(f32[8,32,2048]{2,1,0:T(8,128)} %slice.165), calls=%async_computation | async-start | bytes 4194304 | tf_op jit(solution)/shard_map/all_to_all | solution.py:297
  10.5 2.7 slice.166
  13.2 45.5 %all-to-all-done.series_ref = f32[8,32,2048]{2,1,0:T(8,128)S(1)} async-done(((f32[8,32,2048]{2,1,0:T(8,128)}), f32[8,32,2048]{2,1,0:T(8,128)S(1)}, u32[]{:S(2)}, u32[]{:S(2)}) %all-to-all-start) | async-done | bytes 2097184 | tf_op jit(solution)/shard_map/all_to_all | solution.py:297
  58.8 4.3 %all-to-all-start.2 = ((f32[8,24,2048]{2,1,0:T(8,128)}), f32[8,24,2048]{2,1,0:T(8,128)}, u32[]{:S(2)}, u32[]{:S(2)}) async-start(f32[8,24,2048]{2,1,0:T(8,128)} %slice.166), calls=%async_computation.2 | async-start | bytes 3145728 | tf_op jit(solution)/shard_map/all_to_all | solution.py:297
  65.1 33.7 %shift_sum.3.refs_0_ = f32[64,128,128]{2,1,0:T(8,128)} custom-call(s32[32,64]{1,0:T(8,128)S(1)} %copy.23.delay_ref, f32[8,32,2048]{2,1,0:T(8,128)S(1)} %all-to-all-done.series_ref), custom_call_target="tpu_custom_call" | custom-call | flops 4194304000 | bytes 6291456 | tf_op jit(solution)/shard_map/shift_sum/pallas_call | solution.py:88
  99.7 5.0 %all-to-all-start.1 = ((f32[8,8,2048]{2,1,0:T(8,128)}), f32[8,8,2048]{2,1,0:T(8,128)S(1)}, u32[]{:S(2)}, u32[]{:S(2)}) async-start(f32[8,8,2048]{2,1,0:T(8,128)} %slice.164), calls=%async_computation.1 | async-start | bytes 1048576 | tf_op jit(solution)/shard_map/all_to_all | solution.py:297
  105.0 2.2 copy-done.1
  107.2 25.2 %shift_sum.4.refs_0_ = f32[64,128,128]{2,1,0:T(8,128)S(1)} custom-call(s32[24,64]{1,0:T(8,128)S(1)} %copy.24.delay_ref, f32[8,24,2048]{2,1,0:T(8,128)} %all-to-all-done.2.series_ref, f32[64,128,128]{2,1,0:T(8,128)S(1)} %copy-done.1), custom_call_target="tpu_custom_call", output_to_operand_aliasing={{}: (2, {})} | custom-call | flops 3145728000 | bytes 5767168 | tf_op jit(solution)/shard_map/shift_sum/pallas_call | solution.py:88
  134.4 2.2 copy-done.3
  136.6 9.0 %shift_sum.5 = f32[64,128,128]{2,1,0:T(8,128)S(1)} custom-call(s32[8,64]{1,0:T(8,128)S(1)} %copy.22.delay_ref, f32[8,8,2048]{2,1,0:T(8,128)S(1)} %all-to-all-done.1.series_ref, f32[64,128,128]{2,1,0:T(8,128)S(1)} %copy-done.3), custom_call_target="tpu_custom_call", output_to_operand_aliasing={{}: (2, {})} | custom-call | flops 1048576000 | bytes 4718592 | tf_op jit(solution)/shard_map/shift_sum/pallas_call | solution.py:88
  147.4 2.1 collective-permute-start
  152.0 19.3 %collective-permute-done = f32[2,8,128,128]{3,2,1,0:T(8,128)} collective-permute-done((f32[2,8,128,128]{3,2,1,0:T(8,128)S(1)}, f32[2,8,128,128]{3,2,1,0:T(8,128)}, u32[]{:S(2)}, u32[]{:S(2)}) %collective-permute-start) | collective-permute-done | bytes 1048608 | tf_op jit(solution)/shard_map/ppermute | solution.py:22
  177.7 7.4 %collective-permute-done.1 = f32[8,128,128]{2,1,0:T(8,128)S(1)} collective-permute-done((f32[8,128,128]{2,1,0:T(8,128)S(1)}, f32[8,128,128]{2,1,0:T(8,128)S(1)}, u32[]{:S(2)}, u32[]{:S(2)}) %collective-permute-start.1) | collective-permute-done | bytes 524320 | tf_op jit(solution)/shard_map/ppermute | solution.py:22
  185.1 2.1 collective-permute-done.3
  188.3 4.3 %dft.1 = f32[8,2,9,16,128]{4,3,2,1,0:T(8,128)} custom-call(bf16[384,256]{1,0:T(8,128)(2,1)} %constant.241.clone.first_ref, f32[128,128]{1,0:T(8,128)} %constant.243.clone.twist_cos_ref, f32[128,128]{1,0:T(8,128)} %constant.244.clone.twist_sin_ref, bf16[128,768]{1,0:T(8,128)(2,1)} %constant.242.clone.second_ref, f32[16,128,128]{2,1,0:T(8,128)} %pad_maximum_fusion.series_ref), custom_call_target="tpu_custom_call" | custom-call | tf_op jit(solution)/shard_map/dft/pallas_call | solution.py:200
  192.6 4.7 %all-to-all-start.3 = ((f32[8,2,9,16,128]{4,3,2,1,0:T(8,128)}), f32[8,2,9,16,128]{4,3,2,1,0:T(8,128)S(1)}, u32[]{:S(2)}, u32[]{:S(2)}) async-start(f32[8,2,9,16,128]{4,3,2,1,0:T(8,128)} %dft.1), calls=%async_computation.3 | async-start | bytes 2359296 | tf_op jit(solution)/shard_map/all_to_all | solution.py:315
  198.7 23.9 %all-to-all-done.3 = f32[8,2,9,16,128]{4,3,2,1,0:T(8,128)S(1)} async-done(((f32[8,2,9,16,128]{4,3,2,1,0:T(8,128)}), f32[8,2,9,16,128]{4,3,2,1,0:T(8,128)S(1)}, u32[]{:S(2)}, u32[]{:S(2)}) %all-to-all-start.3) | async-done | bytes 1179680 | tf_op jit(solution)/shard_map/all_to_all | solution.py:315
  223.0 3.1 %fusion.8 = (f32[1,9,128,128]{3,2,1,0:T(8,128)S(1)}, f32[1,9,128,128]{3,2,1,0:T(8,128)S(1)}) fusion(f32[2,9,64,128]{3,2,1,0:T(8,128)S(1)} %get-tuple-element.31, f32[2,9,64,128]{3,2,1,0:T(8,128)S(1)} %get-tuple-element.30, s32[9,128]{1,0:T(8,128)S(1)} %fusion.25, s32[128]{0:T(128)S(1)} %and_select_fusion.4), kind=kLoop, calls=%fused_computation.38 | loop fusion | flops 3981312 | bytes 2364416 | tf_op jit(solution)/shard_map/add | solution.py:38
  227.7 2.5 collective-permute-done.4
  230.5 2.8 slice_add_fusion.1
  237.6 15.8 %collective-permute-done.5 = f32[2,6,128,128]{3,2,1,0:T(8,128)} collective-permute-done((f32[2,6,128,128]{3,2,1,0:T(8,128)S(1)}, f32[2,6,128,128]{3,2,1,0:T(8,128)}, u32[]{:S(2)}, u32[]{:S(2)}) %collective-permute-start.5) | collective-permute-done | bytes 786464 | tf_op jit(solution)/shard_map/ppermute | solution.py:22
  259.0 11.7 %template_search.2.refs_0_ = f32[128,1024]{1,0:T(8,128)} custom-call(f32[32,256]{1,0:T(8,128)S(1)} %select_reduce_fusion.profile_ref, f32[2,6,128,128]{3,2,1,0:T(8,128)S(1)} %pad_maximum_fusion.2.before_ref.tile_ref.after_ref, f32[2,6,128,128]{3,2,1,0:T(8,128)S(1)} %pad_maximum_fusion.2.before_ref.tile_ref.after_ref, ...), custom_call_target="tpu_custom_call" | custom-call | flops 536870912000 | bytes 786432 | tf_op jit(solution)/shard_map/template_search/pallas_call | solution.py:258
  272.9 11.7 %template_search.3 = f32[128,1024]{1,0:T(8,128)} custom-call(f32[32,256]{1,0:T(8,128)S(1)} %select_reduce_fusion.profile_ref, f32[2,6,128,128]{3,2,1,0:T(8,128)S(1)} %pad_maximum_fusion.3.before_ref.tile_ref.after_ref, f32[2,6,128,128]{3,2,1,0:T(8,128)S(1)} %pad_maximum_fusion.3.before_ref.tile_ref.after_ref, ...), custom_call_target="tpu_custom_call", output_to_operand_aliasing={{}: (4, {})} | custom-call | flops 536870912000 | bytes 786432 | tf_op jit(solution)/shard_map/template_search/pallas_call | solution.py:258
  (89 shorter events, 32.5 us)
Async XLA Ops:
  0.0 64.9 %copy-start = (s32[512,64]{0,1:T(8,128)S(1)}, s32[512,64]{0,1:T(8,128)}, u32[]{:S(2)}) copy-start(s32[512,64]{0,1:T(8,128)} %param.10) | copy-start | bytes 393220
  3.2 55.5 %all-to-all-start = ((f32[8,32,2048]{2,1,0:T(8,128)}), f32[8,32,2048]{2,1,0:T(8,128)S(1)}, u32[]{:S(2)}, u32[]{:S(2)}) async-start(f32[8,32,2048]{2,1,0:T(8,128)} %slice.165), calls=%async_computation | async-start | bytes 4194304 | tf_op jit(solution)/shard_map/all_to_all | solution.py:297
  58.8 40.9 %all-to-all-start.2 = ((f32[8,24,2048]{2,1,0:T(8,128)}), f32[8,24,2048]{2,1,0:T(8,128)}, u32[]{:S(2)}, u32[]{:S(2)}) async-start(f32[8,24,2048]{2,1,0:T(8,128)} %slice.166), calls=%async_computation.2 | async-start | bytes 3145728 | tf_op jit(solution)/shard_map/all_to_all | solution.py:297
  99.7 34.7 %all-to-all-start.1 = ((f32[8,8,2048]{2,1,0:T(8,128)}), f32[8,8,2048]{2,1,0:T(8,128)S(1)}, u32[]{:S(2)}, u32[]{:S(2)}) async-start(f32[8,8,2048]{2,1,0:T(8,128)} %slice.164), calls=%async_computation.1 | async-start | bytes 1048576 | tf_op jit(solution)/shard_map/all_to_all | solution.py:297
  105.0 2.2 copy-start.1
  132.5 2.0 copy-start.2
  134.4 2.2 copy-start.3
  145.9 1.4 copy-start.4
  147.4 23.9 %collective-permute-start = (f32[2,8,128,128]{3,2,1,0:T(8,128)S(1)}, f32[2,8,128,128]{3,2,1,0:T(8,128)}, u32[]{:S(2)}, u32[]{:S(2)}) collective-permute-start(f32[2,8,128,128]{3,2,1,0:T(8,128)S(1)} %dynamic-slice_bitcast_fusion.1), channel_id=1, source_target_pairs={{0,1},{1,0},{2,3},{3,2},{4,5},{5,4},{6,7},{7,6},{8,9},{9,8},{10,11... | collective-permute-start | bytes 3145736 | tf_op jit(solution)/shard_map/ppermute | solution.py:22
  150.5 24.2 %collective-permute-start.2 = (f32[2,8,128,128]{3,2,1,0:T(8,128)}, f32[2,8,128,128]{3,2,1,0:T(8,128)}, u32[]{:S(2)}, u32[]{:S(2)}) collective-permute-start(f32[2,8,128,128]{3,2,1,0:T(8,128)} %dynamic-slice_bitcast_fusion), channel_id=1, source_target_pairs={{0,2},{1,3},{2,0},{3,1},{4,6},{5,7},{6,4},{7,5},{8,10},{9,11},{10,... | collective-permute-start | bytes 3145736 | tf_op jit(solution)/shard_map/ppermute | solution.py:22
  173.0 12.1 %collective-permute-start.1 = (f32[8,128,128]{2,1,0:T(8,128)S(1)}, f32[8,128,128]{2,1,0:T(8,128)S(1)}, u32[]{:S(2)}, u32[]{:S(2)}) collective-permute-start(f32[8,128,128]{2,1,0:T(8,128)S(1)} %dynamic-slice_bitcast_fusion.3), channel_id=1, source_target_pairs={{0,2},{1,3},{2,0},{3,1},{4,6},{5,7},{6,4},{7,5},{8,10},{9,11},{10,... | collective-permute-start | bytes 1572872 | tf_op jit(solution)/shard_map/ppermute | solution.py:22
  176.1 11.1 %collective-permute-start.3 = (f32[8,128,128]{2,1,0:T(8,128)S(1)}, f32[8,128,128]{2,1,0:T(8,128)S(1)}, u32[]{:S(2)}, u32[]{:S(2)}) collective-permute-start(f32[8,128,128]{2,1,0:T(8,128)S(1)} %dynamic-slice_bitcast_fusion.2), channel_id=1, source_target_pairs={{0,1},{1,0},{2,3},{3,2},{4,5},{5,4},{6,7},{7,6},{8,9},{9,8},{10,11... | collective-permute-start | bytes 1572872 | tf_op jit(solution)/shard_map/ppermute | solution.py:22
  192.6 4.7 %copy-start.13 = (s32[7]{0:T(128)S(1)}, s32[7]{0:T(128)}, u32[]{:S(2)}) copy-start(s32[7]{0:T(128)} %param.11) | copy-start | bytes 88
  192.6 30.1 %all-to-all-start.3 = ((f32[8,2,9,16,128]{4,3,2,1,0:T(8,128)}), f32[8,2,9,16,128]{4,3,2,1,0:T(8,128)S(1)}, u32[]{:S(2)}, u32[]{:S(2)}) async-start(f32[8,2,9,16,128]{4,3,2,1,0:T(8,128)} %dft.1), calls=%async_computation.3 | async-start | bytes 2359296 | tf_op jit(solution)/shard_map/all_to_all | solution.py:315
  198.7 31.7 %copy-start.7 = (s32[9,128]{1,0:T(8,128)}, s32[9,128]{1,0:T(8,128)S(1)}, u32[]{:S(2)}) copy-start(s32[9,128]{1,0:T(8,128)S(1)} %fusion.25) | copy-start | bytes 13828
  227.2 3.1 %collective-permute-start.4 = (f32[2,9,128,128]{3,2,1,0:T(8,128)}, f32[2,9,128,128]{3,2,1,0:T(8,128)S(1)}, u32[]{:S(2)}, u32[]{:S(2)}) collective-permute-start(f32[2,9,128,128]{3,2,1,0:T(8,128)} %maximum_multiply_fusion), channel_id=1, source_target_pairs={{0,8},{8,0},{16,24},{24,16},{1,9},{9,1},{17,25},{25,17},{2,10},{10... | collective-permute-start | bytes 3538952 | tf_op jit(solution)/shard_map/ppermute | solution.py:22
  233.5 1.6 copy-start.10
  233.5 1.6 copy-start.9
  233.5 3.0 %slice-start.1 = ((s32[9,128]{1,0:T(8,128)}), s32[5,128]{1,0:T(8,128)S(1)}, s32[]{:S(2)}) async-start(s32[9,128]{1,0:T(8,128)} %copy-done.7), calls=%async_computation.5 | async-start | bytes 8192 | tf_op jit(solution)/shard_map/slice | solution.py:355
  233.6 19.8 %collective-permute-start.5 = (f32[2,6,128,128]{3,2,1,0:T(8,128)S(1)}, f32[2,6,128,128]{3,2,1,0:T(8,128)}, u32[]{:S(2)}, u32[]{:S(2)}) collective-permute-start(f32[2,6,128,128]{3,2,1,0:T(8,128)S(1)} %pad_maximum_fusion.1), channel_id=1, source_target_pairs={{0,16},{8,24},{16,0},{24,8},{1,17},{9,25},{17,1},{25,9},{2,18},{10... | collective-permute-start | bytes 2359304 | tf_op jit(solution)/shard_map/ppermute | solution.py:22
  235.9 18.7 %copy-start.11 = (s32[128]{0:T(128)}, s32[128]{0:T(128)S(1)}, u32[]{:S(2)}) copy-start(s32[128]{0:T(128)S(1)} %and_select_fusion) | copy-start | bytes 1540
  257.5 13.1 %collective-permute-start.6 = (f32[2,3,128,128]{3,2,1,0:T(8,128)}, f32[2,3,128,128]{3,2,1,0:T(8,128)}, u32[]{:S(2)}, u32[]{:S(2)}) collective-permute-start(f32[2,3,128,128]{3,2,1,0:T(8,128)} %slice.181), channel_id=1, source_target_pairs={{0,16},{8,24},{16,0},{24,8},{1,17},{9,25},{17,1},{25,9},{2,18},{10... | collective-permute-start | bytes 1179656 | tf_op jit(solution)/shard_map/ppermute | solution.py:22
  270.7 1.2 copy-start.8
  270.7 1.2 copy-start.12
  (3 other events, 3.0 us)
